TPU v7x, 256 devices: a whole 4x4x8 slice. The times are simulated.
256 devices in a mesh: kpt: 32 (over x, y, z_lo), aux: 8 (over z_hi, core).
Axes of the slice: x: 4, y: 4, z: 8 (z_hi: 4, z_lo: 2; z = z_hi * 2 + z_lo), core: 2. Of those that a mesh axis runs over, the one named last changes fastest.
Arguments:
- pair_tensors: bfloat16 [2, 64, 16, 512, 1024], P(None, 'kpt', 'aux'), may hold values from -0.1875 to 0.1875
- orbitals: bfloat16 [64, 512, 512], P('kpt'), may hold values from -6 to 6
- matchings: int32 [2, 64], replicated, may hold values from 0 to 63, as said below
Outputs:
- exchange: float32 [64, 2, 512, 512], P('kpt', None, 'aux')
Inputs may be any that keep to these rules, and one draw needn't show every extreme that they name: Each row matchings[r] is a permutation of the 64 k-points. With 2^m = 32 blocks of 2 consecutive k-points, round r matches every k-point of block d with a k-point of block d XOR 2^(m - 1 - r).
All inputs are finite; a program needn't handle non-finite values.
Results may differ from a plain program's by a relative error of at most 0.00098.
Values may be sent and summed in bfloat16 or wider, within the bound.
A program may use at most 192 MiB of HBM per device.

v0:
```python
import jax
import jax.numpy as jnp
from jax import lax
from jax.sharding import PartitionSpec as P

ROUNDS = 2


def from_partner(shard, axis, distance):
    return lax.ppermute(shard, axis, [(i, i ^ 1 << distance) for i in range(lax.axis_size(axis))])


def build_block(chosen):
    occupied = chosen.shape[-1] // 2
    real_part = chosen[..., :occupied]
    imag_part = chosen[..., occupied:]
    upper_rows = jnp.concatenate([real_part, imag_part], axis=-1)
    bottom = jnp.concatenate([-imag_part, real_part], axis=-1)
    return jnp.concatenate([upper_rows, bottom], axis=-2)


def half_transform(pairs, block):
    return jnp.einsum("kpab,kbc->kpac", pairs, block, preferred_element_type=jnp.float32).astype(
        jnp.bfloat16
    )


def hermitian_rows(left_rows, half_done):
    occupied = half_done.shape[-1] // 2
    rotated = jnp.concatenate([-half_done[..., occupied:], half_done[..., :occupied]], axis=-1)
    exch_real = jnp.einsum(
        "kpac,kpbc->kab", left_rows, half_done, preferred_element_type=jnp.float32
    )
    exch_imag = jnp.einsum("kpac,kpbc->kab", left_rows, rotated, preferred_element_type=jnp.float32)
    return jnp.stack([exch_real, exch_imag], axis=1)


def body(pair_tensors, orbitals, matchings):
    per_device = orbitals.shape[0]
    occupied = orbitals.shape[2] // 2
    bit_count = lax.axis_size("kpt").bit_length() - 1
    factor = 1.0 / (ROUNDS * pair_tensors.shape[2] * lax.axis_size("aux") * occupied) ** 0.5
    offset = lax.axis_index("kpt") * per_device
    collected = []
    for which_round in range(ROUNDS):
        swap_bit = bit_count - 1 - which_round
        partner = from_partner(orbitals, "kpt", swap_bit)
        within = lax.dynamic_slice_in_dim(matchings[which_round], offset, per_device) % per_device
        chosen = jnp.take(partner, within, axis=0)
        half_done = half_transform(pair_tensors[which_round], build_block(chosen))
        pieces = hermitian_rows(half_done, half_done) * factor
        collected.append(pieces)
    running = collected[0]
    for extra in collected[1:]:
        running = running + extra
    running = lax.psum_scatter(running, "aux", scatter_dimension=2, tiled=True)
    return running


def solution(mesh):
    placed = (P(None, "kpt", "aux", None, None), P("kpt", None, None), P())
    return jax.shard_map(
        body, mesh=mesh, in_specs=placed, out_specs=P("kpt", None, "aux", None), check_vma=False
    )
```

profile of v0, /device:TPU:1, one launch (start us, length us, event | category | flops | bytes accessed | tf_op | source)
XLA Modules:
  0.0 140.5 jit_solution(15127794232751463254)
XLA Ops:
  6.5 0.0 reduce-scatter.2.cloned.1.call-start
  6.5 3.6 %collective-permute-start = (bf16[2,512,512]{2,1,0:T(8,128)(2,1)}, bf16[2,512,512]{2,1,0:T(8,128)(2,1)S(1)}, u32[]{:S(2)}, u32[]{:S(2)}) collective-permute-start(bf16[2,512,512]{2,1,0:T(8,128)(2,1)} %param.6), channel_id=1, source_target_pairs={{0,128},{8,136},{16,144},{24,152},{32,160},{40,168},{48,176},{56,1... | collective-permute-start | bytes 3145736 | tf_op jit(solution)/shard_map/ppermute | solution.py:10
  10.1 0.3 collective-permute-start.1
  10.4 0.8 fusion.39
  11.2 0.1 compare_and_fusion
  11.3 0.1 compare_and_fusion.1
  11.4 20.9 %collective-permute-done = bf16[2,512,512]{2,1,0:T(8,128)(2,1)S(1)} collective-permute-done((bf16[2,512,512]{2,1,0:T(8,128)(2,1)}, bf16[2,512,512]{2,1,0:T(8,128)(2,1)S(1)}, u32[]{:S(2)}, u32[]{:S(2)}) %collective-permute-start) | collective-permute-done | bytes 1048608 | tf_op jit(solution)/shard_map/ppermute | solution.py:10
  32.3 0.6 gather_fusion
  32.9 0.5 copy.13
  33.4 0.2 broadcast_select_fusion.1
  33.6 0.1 slice_negate_fusion.3
  33.7 4.6 %convert_bitcast_fusion.1 = bf16[2,2,512,512]{2,3,1,0:T(8,128)(2,1)S(1)} fusion(bf16[2,2,2,512,1024]{4,3,2,1,0:T(8,128)(2,1)} %param.5, bf16[2,512,256]{1,2,0:T(8,128)(2,1)S(1)} %get-tuple-element.17, bf16[2,512,256]{1,2,0:T(8,128)(2,1)S(1)} %get-tuple-element.16, bf16[2,512,512]{1,2,0:T(8,128)(2,1)S(1)} %broadcast_select_fusion.1), kind=kOutput, calls=%fused_computation.29 | convolution fusion | flops 2154823680 | bytes 8388608 | tf_op jit(solution)/shard_map/kpab,kbc->kpac/dot_general | solution.py:23
  38.2 0.0 copy-start
  38.2 1.5 %slice_negate_fusion.1 = (bf16[2,2,512,256]{2,3,1,0:T(8,128)(2,1)}, bf16[2,2,512,256]{2,3,1,0:T(8,128)(2,1)}) fusion(bf16[2,2,512,512]{2,3,1,0:T(8,128)(2,1)S(1)} %convert_bitcast_fusion.1), kind=kLoop, calls=%fused_computation.35 | loop fusion | flops 524288 | bytes 4194304 | tf_op jit(solution)/shard_map/neg | solution.py:30
  39.8 0.4 copy-done
  40.2 2.6 %convolution_bitcast_fusion.1 = f32[2,1,512,512]{3,2,0,1:T(8,128)} fusion(bf16[2,2,512,512]{2,3,1,0:T(8,128)(2,1)S(1)} %convert_bitcast_fusion.1), kind=kOutput, calls=%fused_computation.33 | convolution fusion | flops 1073741824 | bytes 4194304 | tf_op jit(solution)/shard_map/kpac,kpbc->kab/dot_general | solution.py:31
  42.9 12.8 %collective-permute-done.1 = bf16[2,512,512]{2,1,0:T(8,128)(2,1)S(1)} collective-permute-done((bf16[2,512,512]{2,1,0:T(8,128)(2,1)}, bf16[2,512,512]{2,1,0:T(8,128)(2,1)S(1)}, u32[]{:S(2)}, u32[]{:S(2)}) %collective-permute-start.1) | collective-permute-done | bytes 1048608 | tf_op jit(solution)/shard_map/ppermute | solution.py:10
  55.7 0.6 gather_fusion.1
  56.3 0.5 copy.18
  56.8 0.2 broadcast_select_fusion
  57.0 0.1 slice_negate_fusion.2
  57.1 4.6 %convert_bitcast_fusion = bf16[2,2,512,512]{2,3,1,0:T(8,128)(2,1)S(1)} fusion(bf16[2,2,2,512,1024]{4,3,2,1,0:T(8,128)(2,1)} %param.5, bf16[2,512,256]{1,2,0:T(8,128)(2,1)S(1)} %get-tuple-element.15, bf16[2,512,256]{1,2,0:T(8,128)(2,1)S(1)} %get-tuple-element.14, bf16[2,512,512]{1,2,0:T(8,128)(2,1)S(1)} %broadcast_select_fusion), kind=kOutput, calls=%fused_computation.28 | convolution fusion | flops 2154823680 | bytes 8388608 | tf_op jit(solution)/shard_map/kpab,kbc->kpac/dot_general | solution.py:23
  61.7 1.3 convolution_bitcast_fusion
  63.0 0.0 copy-start.1
  63.0 0.0 copy-start.3
  63.0 0.0 copy-start.4
  63.0 0.1 slice_negate_fusion
  63.1 1.4 %copy-done.1 = bf16[2,2,512,512]{2,3,1,0:T(8,128)(2,1)S(1)} copy-done((bf16[2,2,512,512]{2,3,1,0:T(8,128)(2,1)S(1)}, bf16[2,2,512,512]{2,3,1,0:T(8,128)(2,1)}, u32[]{:S(2)}) %copy-start.1) | copy-done | bytes 2097176
  64.5 0.3 copy-done.3
  64.8 0.3 copy-done.4
  65.1 1.3 fusion.30
  66.4 0.0 copy-start.2
  66.4 1.3 fusion.27
  67.7 0.3 copy-done.2
  68.0 3.0 %fusion = f32[2,2,512,512]{3,2,0,1:T(8,128)} fusion(f32[2,1,512,512]{3,2,0,1:T(8,128)S(1)} %fusion.30, f32[2,1,512,512]{3,2,0,1:T(8,128)S(1)} %copy-done.2, f32[2,1,512,512]{3,2,0,1:T(8,128)S(1)} %fusion.27, f32[2,1,512,512]{3,2,0,1:T(8,128)S(1)} %convolution_bitcast_fusion), kind=kLoop, calls=%fused_computation.3 | loop fusion | flops 4194304 | bytes 12582912 | tf_op jit(solution)/shard_map/add | solution.py:55
  71.0 0.0 reduce-scatter.2.cloned.1.call-update
  71.0 60.8 %reduce-scatter.2.cloned.1.call-done = f32[2,2,64,512]{3,2,0,1:T(8,128)} async-done(((f32[2,2,512,512]{3,2,0,1:T(8,128)}), f32[2,2,64,512]{3,2,0,1:T(8,128)}) %reduce-scatter.2.cloned.1.call-update) | async-done | bytes 524304 | tf_op jit(solution)/shard_map/reduce_scatter | solution.py:56
  131.8 1.9 %copy.23 = f32[2,2,64,512]{3,2,1,0:T(8,128)} copy(f32[2,2,64,512]{3,2,0,1:T(8,128)} %reduce-scatter.2.cloned.1.call-done) | data formatting | bytes 1048576 | tf_op jit(solution)/shard_map/reduce_scatter | solution.py:56
  (2 shorter events, 0.0 us)
Async XLA Ops:
  6.5 125.3 %reduce-scatter.2.cloned.1.call-start = ((), (), s32[]{:S(2)}) async-start(), calls=%async_computation.1 | async-start | bytes 4718592 | tf_op jit(solution)/shard_map/reduce_scatter | solution.py:56
  6.5 25.7 %collective-permute-start = (bf16[2,512,512]{2,1,0:T(8,128)(2,1)}, bf16[2,512,512]{2,1,0:T(8,128)(2,1)S(1)}, u32[]{:S(2)}, u32[]{:S(2)}) collective-permute-start(bf16[2,512,512]{2,1,0:T(8,128)(2,1)} %param.6), channel_id=1, source_target_pairs={{0,128},{8,136},{16,144},{24,152},{32,160},{40,168},{48,176},{56,1... | collective-permute-start | bytes 3145736 | tf_op jit(solution)/shard_map/ppermute | solution.py:10
  10.1 45.6 %collective-permute-start.1 = (bf16[2,512,512]{2,1,0:T(8,128)(2,1)}, bf16[2,512,512]{2,1,0:T(8,128)(2,1)S(1)}, u32[]{:S(2)}, u32[]{:S(2)}) collective-permute-start(bf16[2,512,512]{2,1,0:T(8,128)(2,1)} %param.6), channel_id=1, source_target_pairs={{0,64},{8,72},{16,80},{24,88},{32,96},{40,104},{48,112},{56,120},{... | collective-permute-start | bytes 3145736 | tf_op jit(solution)/shard_map/ppermute | solution.py:10
  38.2 2.0 %copy-start = (bf16[2,2,512,512]{2,3,1,0:T(8,128)(2,1)}, bf16[2,2,512,512]{2,3,1,0:T(8,128)(2,1)S(1)}, u32[]{:S(2)}) copy-start(bf16[2,2,512,512]{2,3,1,0:T(8,128)(2,1)S(1)} %convert_bitcast_fusion.1) | copy-start | bytes 6291460
  63.0 1.6 %copy-start.1 = (bf16[2,2,512,512]{2,3,1,0:T(8,128)(2,1)S(1)}, bf16[2,2,512,512]{2,3,1,0:T(8,128)(2,1)}, u32[]{:S(2)}) copy-start(bf16[2,2,512,512]{2,3,1,0:T(8,128)(2,1)} %copy-done) | copy-start | bytes 6291460
  63.0 1.8 %copy-start.3 = (bf16[2,2,512,256]{2,3,1,0:T(8,128)(2,1)S(1)}, bf16[2,2,512,256]{2,3,1,0:T(8,128)(2,1)}, u32[]{:S(2)}) copy-start(bf16[2,2,512,256]{2,3,1,0:T(8,128)(2,1)} %get-tuple-element.12) | copy-start | bytes 3145732
  63.0 2.2 %copy-start.4 = (bf16[2,2,512,256]{2,3,1,0:T(8,128)(2,1)S(1)}, bf16[2,2,512,256]{2,3,1,0:T(8,128)(2,1)}, u32[]{:S(2)}) copy-start(bf16[2,2,512,256]{2,3,1,0:T(8,128)(2,1)} %get-tuple-element.13) | copy-start | bytes 3145732
  66.4 1.6 %copy-start.2 = (f32[2,1,512,512]{3,2,0,1:T(8,128)S(1)}, f32[2,1,512,512]{3,2,0,1:T(8,128)}, u32[]{:S(2)}) copy-start(f32[2,1,512,512]{3,2,0,1:T(8,128)} %convolution_bitcast_fusion.1) | copy-start | bytes 6291460
Sparse Core Ops, SparseCore 0:
  71.1 60.6 reduce-scatter.1
where the time goes:
time: 142 us; the launch traced here: 141 us
  waiting for transfers between devices  94.5 us (67%)
  matrix products  15.6 us (11%)
  between operations  13.5 us (10%)
  local copies, waits for them, and re-layouts  7.67 us (5%)
  other arithmetic  5.32 us (4%)
  starting transfers between devices  3.89 us (3%)
    reduce_scatter x1, waiting for transfers between devices, body(): running = lax.psum_scatter(running, 'aux', scatter_dimension=2, tiled=True)  60.8 us
    ppermute x2, waiting for transfers between devices, from_partner(): lax.ppermute(shard, axis, [(i, i ^ 1 << distance) for i in range(lax.axis...  33.7 us
    dot_general x2, matrix products, half_transform(): jnp.einsum('kpab,kbc->kpac', pairs, block, preferred_element_type=jnp.flo...  9.11 us
    dot_general x2, matrix products, hermitian_rows(): jnp.einsum('kpac,kpbc->kab', left_rows, half_done, preferred_element_type...  3.91 us
    ppermute x2, starting transfers between devices, from_partner(): lax.ppermute(shard, axis, [(i, i ^ 1 << distance) for i in range(lax.axis...  3.89 us
    add x1, other arithmetic, body(): running = running + extra  2.98 us
  transfers between devices with their start and end apart: 3, of which 3 were waited for; matrix products, arithmetic and copies ran while one was open for 8% of the time, Pallas kernels for 0%

commit v1 on v0

v1 whole, which is shorter than its diff:
```python
import functools

import jax
import jax.numpy as jnp
from jax import lax
from jax.experimental import pallas as pl
from jax.experimental.pallas import tpu as pltpu
from jax.sharding import PartitionSpec as P

MESH = pl.DeviceIdType.MESH
ROUNDS = 2
LEVELS = 32000.0
SMALLEST = 1e-30
PIECES = 4


def kernel(
    factor, pairs, orbs, match, out,
    held_pairs, c00, c01, c10, c11, block, halves, squares, scale_rows, scale_cols,
    codes, codes_in, scales, scales_in, total, handed,
    pair_sem, pair_send, pair_recv, x_send, x_recv, relay_send, relay_recv,
    share_send, share_recv, code_send, code_recv, scale_send, scale_recv, hand_send, hand_recv,
):
    kpt, aux = lax.axis_index("kpt"), lax.axis_index("aux")
    chip, core = aux // 2, aux % 2
    x = kpt // 8
    rest = kpt - x * 8
    near = (x + 1 - 2 * (x % 2)) * 8 + rest
    cross = (3 - x) * 8 + rest
    sibling = aux + 1 - 2 * core
    here = (kpt, sibling)
    nao, nocc = orbs.shape[1], orbs.shape[2] // 2
    width = nocc // 2
    rows = nao // PIECES
    naux = pairs.shape[2]
    combos = 2 * naux
    chosen = ((c00, c01), (c10, c11))

    def remote(src, dst, send, recv, device):
        return pltpu.make_async_remote_copy(
            src_ref=src, dst_ref=dst, send_sem=send, recv_sem=recv, device_id=device, device_id_type=MESH
        )

    def own_pair(r, p):
        return pltpu.make_async_copy(
            pairs.at[r, core, p], held_pairs.at[r, core * naux + p], pair_sem.at[r, p]
        )

    def given_pair(r, p):
        return remote(
            pairs.at[r, 1 - core, p], held_pairs.at[r, core * naux + p],
            pair_send.at[r, p], pair_recv.at[r, p], here,
        )

    def x_piece(q, t, part):
        return remote(
            orbs.at[core, pl.ds(t * rows, rows), pl.ds(part * nocc + q * width, width)],
            chosen[1][q].at[core, pl.ds(t * rows, rows), pl.ds(part * width, width)],
            x_send.at[q, t, part], x_recv.at[q, t, part], (near, aux),
        )

    def relay(q, t):
        return remote(
            chosen[1][q].at[core, pl.ds(t * rows, rows)], chosen[0][q].at[core, pl.ds(t * rows, rows)],
            relay_send.at[q, t], relay_recv.at[q, t], (cross, aux),
        )

    def share(r, q):
        return remote(
            chosen[r][q].at[core], chosen[r][q].at[core], share_send.at[r, q], share_recv.at[r, q], here
        )

    for r in (1, 0):
        for p in range(naux):
            own_pair(r, p).start()

    barrier = pltpu.get_barrier_semaphore()
    peers = [(kpt, lax.rem(chip + d, 4) * 2 + core) for d in (1, 2, 3)]
    for device in [(near, aux), (cross, aux), here] + peers:
        pl.semaphore_signal(barrier, inc=1, device_id=device, device_id_type=MESH)
    pl.semaphore_wait(barrier, 6)

    for q in range(2):
        for t in range(PIECES):
            for part in range(2):
                x_piece(q, t, part).start()
    for r in (1, 0):
        for p in range(naux):
            given_pair(r, p).start()
    squares[...] = jnp.zeros_like(squares)

    def pass_on(q, t):
        for part in range(2):
            x_piece(q, t, part).wait_recv()
        relay(q, t).start()

    def build(r, q):
        index = jnp.bitwise_and(match[r, kpt * 2 + core], 1)
        both = chosen[r][q][index]
        block[0:nao, :] = both
        block[nao:, 0:width] = -both[:, width:]
        block[nao:, width:] = both[:, 0:width]

    def transform(r, q, first, last):
        def step(p, carry):
            done = jnp.dot(held_pairs[r, p], block[...], preferred_element_type=jnp.float32).astype(jnp.bfloat16)
            real, imag = done[:, 0:width], done[:, width:]
            at = pl.multiple_of((r * combos + p) * 2 * nocc + q * 2 * width, 2 * width)
            halves[0:nao, pl.ds(at, 2 * width)] = done
            halves[nao:, pl.ds(at, 2 * width)] = jnp.concatenate([-imag, real], axis=1)
            wide_real, wide_imag = real.astype(jnp.float32), imag.astype(jnp.float32)
            squares[...] += wide_real * wide_real + wide_imag * wide_imag
            return carry

        lax.fori_loop(first, last, step, 0)

    for t in range(PIECES):
        pass_on(0, t)
    share(1, 0).start()
    for p in range(naux):
        own_pair(1, p).wait()
    for p in range(naux):
        given_pair(1, p).wait_recv()
    share(1, 0).wait_recv()
    build(1, 0)
    transform(1, 0, 0, naux)
    pass_on(1, 0)
    transform(1, 0, naux, combos)
    for t in range(PIECES):
        relay(0, t).wait_recv()
    share(0, 0).start()
    pass_on(1, 1)
    for p in range(naux):
        own_pair(0, p).wait()
    for p in range(naux):
        given_pair(0, p).wait_recv()
    share(0, 0).wait_recv()
    build(0, 0)
    transform(0, 0, 0, naux)
    pass_on(1, 2)
    transform(0, 0, naux, combos)
    pass_on(1, 3)
    share(1, 1).start()
    share(1, 1).wait_recv()
    build(1, 1)
    transform(1, 1, 0, combos)
    for t in range(PIECES):
        relay(1, t).wait_recv()
    share(0, 1).start()
    share(0, 1).wait_recv()
    build(0, 1)
    transform(0, 1, 0, combos)

    length = jnp.sqrt(jnp.maximum(jnp.sum(squares[...], axis=1, keepdims=True), SMALLEST))
    spread = jnp.broadcast_to(length, (nao, 128))
    gain = LEVELS ** 0.5
    scale_cols[...] = gain / spread
    for j in range(4):
        turned = spread[j * 128 : (j + 1) * 128, :].T[0:8, :]
        scales[:, j * 128 : (j + 1) * 128] = turned
        scale_rows[:, j * 128 : (j + 1) * 128] = gain / turned

    def offset(step):
        return 2 - step + 3 * (step // 2)

    def peer(step):
        return (kpt, lax.rem(chip + offset(step), 4) * 2 + core)

    def send_codes(step, part):
        return remote(
            codes.at[step, part], codes_in.at[step, part],
            code_send.at[step, part], code_recv.at[step, part], peer(step),
        )

    def send_scales(step):
        return remote(scales, scales_in.at[step], scale_send.at[step], scale_recv.at[step], peer(step))

    for step in range(3):
        send_scales(step).start()

    def products(owner, part):
        mine = halves[pl.ds(pl.multiple_of(owner * 128, 128), 128), :]
        return lax.dot_general(
            halves[part * nao : (part + 1) * nao, :], mine, (((1,), (1,)), ((), ())),
            preferred_element_type=jnp.float32,
        )

    def term(step, carry):
        owner = lax.rem(chip + offset(step), 4)
        down = scale_cols[pl.ds(pl.multiple_of(owner * 128, 128), 128), :]
        for part in range(2):
            sums = products(owner, part)
            for j in range(4):
                cols = slice(j * 128, (j + 1) * 128)
                scaled = sums[cols, :].T * down * scale_rows[0:1, cols]
                codes[step, part, :, cols] = jnp.round(scaled).astype(jnp.int32).astype(jnp.int16)
            send_codes(step, part).start()
        return carry

    lax.fori_loop(0, 3, term, 0)
    for part in range(2):
        sums = products(chip, part)
        for j in range(4):
            cols = slice(j * 128, (j + 1) * 128)
            total[part, :, cols] = sums[cols, :].T * factor

    def hand():
        return remote(handed, out.at[core], hand_send, hand_recv, here)

    for step in range(3):
        send_scales(step).wait()
        across = scales_in[step] * (factor / LEVELS)
        mine = jnp.broadcast_to(scales_in[step, 0:1, pl.ds(pl.multiple_of(chip * 128, 128), 128)], (128, 128)).T
        for part in range(2):
            send_codes(step, part).wait()
            for j in range(4):
                cols = slice(j * 128, (j + 1) * 128)
                wide = codes_in[step, part, :, cols].astype(jnp.int32).astype(jnp.float32)
                total[part, :, cols] += wide * mine * across[0:1, cols]
    for part in range(2):
        handed[part] = total[part, pl.ds(pl.multiple_of((1 - core) * 64, 64), 64), :]
    hand().start()
    for part in range(2):
        out[core, part] = total[part, pl.ds(pl.multiple_of(core * 64, 64), 64), :]

    for q in range(2):
        for t in range(PIECES):
            for part in range(2):
                x_piece(q, t, part).wait_send()
            relay(q, t).wait_send()
        for r in range(2):
            share(r, q).wait_send()
    for r in range(2):
        for p in range(naux):
            given_pair(r, p).wait_send()
    hand().wait()


def body(pairs, orbs, match):
    rounds, per_device, naux, nao, _ = pairs.shape
    nocc = orbs.shape[2] // 2
    factor = 1.0 / (rounds * naux * lax.axis_size("aux") * nocc) ** 0.5
    dma = pltpu.SemaphoreType.DMA
    combos = 2 * naux
    orbital_chunk = pltpu.VMEM((per_device, nao, nocc), jnp.bfloat16)
    return pl.pallas_call(
        functools.partial(kernel, factor),
        out_shape=jax.ShapeDtypeStruct((per_device, 2, nao // 8, nao), jnp.float32),
        in_specs=[
            pl.BlockSpec(memory_space=pl.ANY),
            pl.BlockSpec(memory_space=pl.ANY),
            pl.BlockSpec(memory_space=pltpu.SMEM),
        ],
        out_specs=pl.BlockSpec(memory_space=pltpu.VMEM),
        scratch_shapes=[
            pltpu.VMEM((rounds, combos, nao, 2 * nao), jnp.bfloat16),
            orbital_chunk, orbital_chunk, orbital_chunk, orbital_chunk,
            pltpu.VMEM((2 * nao, nocc), jnp.bfloat16),
            pltpu.VMEM((2 * nao, rounds * combos * 2 * nocc), jnp.bfloat16),
            pltpu.VMEM((nao, 128), jnp.float32),
            pltpu.VMEM((8, nao), jnp.float32),
            pltpu.VMEM((nao, 128), jnp.float32),
            pltpu.VMEM((3, 2, 128, nao), jnp.int16),
            pltpu.VMEM((3, 2, 128, nao), jnp.int16),
            pltpu.VMEM((8, nao), jnp.float32),
            pltpu.VMEM((3, 8, nao), jnp.float32),
            pltpu.VMEM((2, 128, nao), jnp.float32),
            pltpu.VMEM((2, 64, nao), jnp.float32),
            dma((rounds, naux)), dma((rounds, naux)), dma((rounds, naux)),
            dma((2, PIECES, 2)), dma((2, PIECES, 2)), dma((2, PIECES)), dma((2, PIECES)),
            dma((2, 2)), dma((2, 2)), dma((3, 2)), dma((3, 2)), dma((3,)), dma((3,)), dma, dma,
        ],
        compiler_params=pltpu.CompilerParams(
            collective_id=0, has_side_effects=True, vmem_limit_bytes=56 << 20
        ),
    )(pairs, orbs, match)


def solution(mesh):
    placed = (P(None, "kpt", "aux", None, None), P("kpt", None, None), P())
    return jax.shard_map(
        body, mesh=mesh, in_specs=placed, out_specs=P("kpt", None, "aux", None), check_vma=False
    )
```

time: 142 us -> 65.8 us (0.46)
  waiting for transfers between devices: 94.5 us -> 0 us
  Pallas kernels: 0 us -> 63.8 us
  matrix products: 15.6 us -> 0 us
  between operations: 13.5 us -> 0.01 us
  local copies, waits for them, and re-layouts: 7.67 us -> 1.87 us
  other arithmetic: 5.32 us -> 0 us
  starting transfers between devices: 3.89 us -> 0 us
    pallas_call x0 -> x1, Pallas kernels: none -> 63.8 us  [body(): pl.pallas_call(functools.partial(kernel, factor), out_shape=jax.ShapeDtyp...]
    reduce_scatter x1 -> x0, waiting for transfers between devices: 60.8 us -> none  [body(): running = lax.psum_scatter(running, 'aux', scatter_dimension=2, tiled=True)]
    ppermute x2 -> x0, waiting for transfers between devices: 33.7 us -> none  [from_partner(): lax.ppermute(shard, axis, [(i, i ^ 1 << distance) for i in range(lax.axis...]
    dot_general x6 -> x0, matrix products: 15.6 us -> none  [the longest x2 9.11 us: half_transform(): jnp.einsum('kpab,kbc->kpac', pairs, block, preferred_element_type=jnp.flo...]
    ppermute x2 -> x0, starting transfers between devices: 3.89 us -> none  [from_partner(): lax.ppermute(shard, axis, [(i, i ^ 1 << distance) for i in range(lax.axis...]
    add x1 -> x0, other arithmetic: 2.98 us -> none  [body(): running = running + extra]
    gather x4 -> x0, local copies, waits for them, and re-layouts: 2.31 us -> none  [body(): chosen = jnp.take(partner, within, axis=0)]
    reduce_scatter x1 -> x0, local copies, waits for them, and re-layouts: 1.87 us -> none  [body(): running = lax.psum_scatter(running, 'aux', scatter_dimension=2, tiled=True)]
  transfers between devices with their start and end apart: 3 -> 0, of which waited for: 3 -> 0; matrix products, arithmetic and copies ran while one was open for 8% -> 0% of each run, Pallas kernels for 0% -> 0%
where the time goes in v1:
time: 65.8 us; the launch traced here: 65.7 us
  Pallas kernels  63.8 us (97%)
  local copies, waits for them, and re-layouts  1.87 us (3%)
    pallas_call x1, Pallas kernels, body(): pl.pallas_call(functools.partial(kernel, factor), out_shape=jax.ShapeDtyp...  63.8 us
    unnamed x1, local copies, waits for them, and re-layouts  1.87 us

profile of v1, /device:TPU:1, one launch (start us, length us, event | category | flops | bytes accessed | tf_op | source)
XLA Modules:
  0.0 65.7 jit_solution(32125786055017532)
XLA Ops:
  0.0 63.8 %shard_map.37 = f32[2,2,64,512]{3,2,1,0:T(8,128)} custom-call(bf16[2,2,2,512,1024]{4,3,2,1,0:T(8,128)(2,1)} %pairs.1, bf16[2,512,512]{2,1,0:T(8,128)(2,1)} %orbs.1, s32[2,64]{1,0:T(2,128)} %match.1), custom_call_target="tpu_custom_call" | custom-call | tf_op jit(solution)/shard_map/pallas_call | solution.py:246
  63.8 1.9 %copy.5 = f32[2,2,64,512]{3,2,1,0:T(8,128)} copy(f32[2,2,64,512]{3,2,1,0:T(8,128)} %shard_map.37) | data formatting | bytes 1048576

commit v2 on v1

--- a/solution.py
+++ b/solution.py
@@ -16,10 +16,11 @@
 
 def kernel(
     factor, pairs, orbs, match, out,
-    held_pairs, c00, c01, c10, c11, block, halves, squares, scale_rows, scale_cols,
-    codes, codes_in, scales, scales_in, total, handed,
+    held_pairs, c00, c01, c10, c11, block, halves, squares, scale_cols,
+    codes, codes_in, scales, scales_in, sums_scale, other_scale, turned, total, sums, sums_in, handed,
     pair_sem, pair_send, pair_recv, x_send, x_recv, relay_send, relay_recv,
-    share_send, share_recv, code_send, code_recv, scale_send, scale_recv, hand_send, hand_recv,
+    share_send, share_recv, code_send, code_recv, scale_send, scale_recv, share_scale_sem,
+    sum_send, sum_recv, hand_send, hand_recv,
 ):
     kpt, aux = lax.axis_index("kpt"), lax.axis_index("aux")
     chip, core = aux // 2, aux % 2
@@ -33,6 +34,7 @@
     width = nocc // 2
     rows = nao // PIECES
     naux = pairs.shape[2]
+    tile = nao // 4
     combos = 2 * naux
     chosen = ((c00, c01), (c10, c11))
 
@@ -75,10 +77,10 @@
             own_pair(r, p).start()
 
     barrier = pltpu.get_barrier_semaphore()
-    peers = [(kpt, lax.rem(chip + d, 4) * 2 + core) for d in (1, 2, 3)]
+    peers = [(kpt, lax.rem(chip + d, 4) * 2 + side) for d in (1, 2, 3) for side in range(2)]
     for device in [(near, aux), (cross, aux), here] + peers:
         pl.semaphore_signal(barrier, inc=1, device_id=device, device_id_type=MESH)
-    pl.semaphore_wait(barrier, 6)
+    pl.semaphore_wait(barrier, 9)
 
     for q in range(2):
         for t in range(PIECES):
@@ -151,14 +153,15 @@
     build(0, 1)
     transform(0, 1, 0, combos)
 
+    gain = LEVELS ** 0.5
     length = jnp.sqrt(jnp.maximum(jnp.sum(squares[...], axis=1, keepdims=True), SMALLEST))
-    spread = jnp.broadcast_to(length, (nao, 128))
-    gain = LEVELS ** 0.5
+    spread = jnp.broadcast_to(length, (nao, tile))
     scale_cols[...] = gain / spread
     for j in range(4):
-        turned = spread[j * 128 : (j + 1) * 128, :].T[0:8, :]
-        scales[:, j * 128 : (j + 1) * 128] = turned
-        scale_rows[:, j * 128 : (j + 1) * 128] = gain / turned
+        scales[:, j * tile : (j + 1) * tile] = spread[j * tile : (j + 1) * tile, :].T[0:8, :]
+
+    def place(j):
+        return pl.ds(pl.multiple_of(lax.rem(j, 4) * tile, tile), tile)
 
     def offset(step):
         return 2 - step + 3 * (step // 2)
@@ -166,63 +169,145 @@
     def peer(step):
         return (kpt, lax.rem(chip + offset(step), 4) * 2 + core)
 
-    def send_codes(step, part):
-        return remote(
-            codes.at[step, part], codes_in.at[step, part],
-            code_send.at[step, part], code_recv.at[step, part], peer(step),
-        )
-
     def send_scales(step):
         return remote(scales, scales_in.at[step], scale_send.at[step], scale_recv.at[step], peer(step))
 
+    def share_scales():
+        return remote(sums_scale, other_scale, share_scale_sem.at[0], share_scale_sem.at[1], here)
+
     for step in range(3):
         send_scales(step).start()
 
-    def products(owner, part):
-        mine = halves[pl.ds(pl.multiple_of(owner * 128, 128), 128), :]
+    def sources(owner):
+        return (
+            (lax.rem(owner + 1, 4), 0), (lax.rem(owner + 3, 4), 1), (lax.rem(owner + 2, 4), owner // 2),
+        )
+
+    def product(owner, j, part):
+        left = halves[pl.ds(pl.multiple_of(part * nao + j * tile, tile), tile), :]
         return lax.dot_general(
-            halves[part * nao : (part + 1) * nao, :], mine, (((1,), (1,)), ((), ())),
-            preferred_element_type=jnp.float32,
-        )
-
-    def term(step, carry):
+            left, halves[place(owner), :], (((1,), (1,)), ((), ())), preferred_element_type=jnp.float32
+        )
+
+    below = lax.broadcasted_iota(jnp.int32, (tile, tile), 0) >= lax.broadcasted_iota(jnp.int32, (tile, tile), 1)
+
+    def diagonal(owner):
+        return jnp.where(below, product(owner, owner, 0), product(owner, owner, 1))
+
+    def coded(value, rows_scale, cols_scale):
+        return jnp.round(value * rows_scale * cols_scale).astype(jnp.int32).astype(jnp.int16)
+
+    def send_codes(step, unit):
+        return remote(
+            codes.at[step, unit], codes_in.at[step, unit],
+            code_send.at[step, unit], code_recv.at[step, unit], peer(step),
+        )
+
+    def send_blocks(step, carry):
         owner = lax.rem(chip + offset(step), 4)
-        down = scale_cols[pl.ds(pl.multiple_of(owner * 128, 128), 128), :]
-        for part in range(2):
-            sums = products(owner, part)
-            for j in range(4):
-                cols = slice(j * 128, (j + 1) * 128)
-                scaled = sums[cols, :].T * down * scale_rows[0:1, cols]
-                codes[step, part, :, cols] = jnp.round(scaled).astype(jnp.int32).astype(jnp.int16)
-            send_codes(step, part).start()
+        for unit, (j, part) in enumerate(sources(owner)):
+            value = product(owner, j, part)
+            codes[step, unit] = coded(value.T, scale_cols[place(owner), :], gain / scales[0:1, place(j)])
+            send_codes(step, unit).start()
         return carry
 
-    lax.fori_loop(0, 3, term, 0)
-    for part in range(2):
-        sums = products(chip, part)
-        for j in range(4):
-            cols = slice(j * 128, (j + 1) * 128)
-            total[part, :, cols] = sums[cols, :].T * factor
-
-    def hand():
-        return remote(handed, out.at[core], hand_send, hand_recv, here)
-
+    def send_diagonal(step, carry):
+        owner = lax.rem(chip + offset(step), 4)
+        value = diagonal(owner)
+        codes[step, 3] = coded(value.T, scale_cols[place(owner), :], gain / scales[0:1, place(owner)])
+        send_codes(step, 3).start()
+        return carry
+
+    lax.fori_loop(0, 3, send_blocks, 0)
+    for unit, (j, part) in enumerate(sources(chip)):
+        total[unit] = product(chip, j, part).T
+    lax.fori_loop(0, 3, send_diagonal, 0)
+    total[3] = diagonal(chip).T
+
+    summed = scales[...] * scales[...]
     for step in range(3):
         send_scales(step).wait()
-        across = scales_in[step] * (factor / LEVELS)
-        mine = jnp.broadcast_to(scales_in[step, 0:1, pl.ds(pl.multiple_of(chip * 128, 128), 128)], (128, 128)).T
-        for part in range(2):
-            send_codes(step, part).wait()
-            for j in range(4):
-                cols = slice(j * 128, (j + 1) * 128)
-                wide = codes_in[step, part, :, cols].astype(jnp.int32).astype(jnp.float32)
-                total[part, :, cols] += wide * mine * across[0:1, cols]
-    for part in range(2):
-        handed[part] = total[part, pl.ds(pl.multiple_of((1 - core) * 64, 64), 64), :]
-    hand().start()
-    for part in range(2):
-        out[core, part] = total[part, pl.ds(pl.multiple_of(core * 64, 64), 64), :]
-
+        summed += scales_in[step] * scales_in[step]
+        received = scales_in[step, 0:1, place(chip)]
+        turned[step] = jnp.broadcast_to(received, (tile, tile)).T * (1.0 / LEVELS)
+    sums_scale[...] = jnp.sqrt(summed)
+    share_scales().start()
+    own_turned = jnp.broadcast_to(sums_scale[0:1, place(chip)], (tile, tile)).T
+
+    def gather(step, unit, j):
+        send_codes(step, unit).wait()
+        wide = codes_in[step, unit].astype(jnp.int32).astype(jnp.float32)
+        total[unit] += wide * turned[step] * scales_in[step, 0:1, place(j)]
+
+    def send_sum(unit, side):
+        j = sources(chip)[unit][0]
+        return remote(
+            sums.at[unit, pl.ds(side * 64, 64)], sums_in.at[core, unit],
+            sum_send.at[unit, side], sum_recv.at[core, unit], (kpt, j * 2 + side),
+        )
+
+    def take_sum(k, unit):
+        return remote(
+            sums.at[unit, pl.ds(0, 64)], sums_in.at[k, unit], sum_send.at[unit, 0], sum_recv.at[k, unit], here
+        )
+
+    for unit, (j, part) in enumerate(sources(chip)):
+        for step in range(3):
+            gather(step, unit, j)
+        sums[unit] = coded(
+            (total[unit] * (gain / own_turned) * (gain / sums_scale[0:1, place(j)])).T, 1.0, 1.0
+        )
+        for side in range(2):
+            send_sum(unit, side).start()
+
+    def hand(unit, part, j):
+        return remote(
+            handed.at[unit], out.at[core, part, :, place(j)], hand_send.at[unit], hand_recv.at[unit], here
+        )
+
+    mine = pl.ds(pl.multiple_of(core * 64, 64), 64)
+    theirs = pl.ds(pl.multiple_of((1 - core) * 64, 64), 64)
+    final = [(unit, part, j) for unit, (j, part) in enumerate(sources(chip))]
+    final += [(3, 0, chip), (4, 1, chip)]
+    for unit, part, j in final[:3]:
+        handed[unit] = total[unit, theirs, :] * factor
+        hand(unit, part, j).start()
+        out[core, part, :, place(j)] = total[unit, mine, :] * factor
+    for step in range(3):
+        gather(step, 3, chip)
+    packed = total[3] * factor
+    turned[0] = packed.T
+    strict = lax.broadcasted_iota(jnp.int32, (tile, tile), 0) > lax.broadcasted_iota(jnp.int32, (tile, tile), 1)
+    real = jnp.where(strict, turned[0], packed)
+    imag = jnp.where(strict, packed, 0.0)
+    total[3] = real
+    total[4] = imag - imag.T
+    for unit, part, j in final[3:]:
+        handed[unit] = total[unit, theirs, :]
+        hand(unit, part, j).start()
+        out[core, part, :, place(j)] = total[unit, mine, :]
+
+    share_scales().wait()
+    for same in range(2):
+        k = core if same == 1 else 1 - core
+        scale = sums_scale if same == 1 else other_scale
+        block_rows = jnp.broadcast_to(scale[0:1, place(chip)], (tile, tile)).T * (factor / LEVELS)
+        turned[same] = block_rows
+        down = turned[same, mine, :]
+        for unit, (j, part) in enumerate(
+            ((lax.rem(chip + 3, 4), 0), (lax.rem(chip + 1, 4), 1), (lax.rem(chip + 2, 4), 1 - chip // 2))
+        ):
+            take_sum(k, unit).wait_recv()
+            wide = sums_in[k, unit].astype(jnp.int32).astype(jnp.float32)
+            sign = 1 - 2 * part
+            value = wide * down * scale[0:1, place(j)]
+            out[k, part, :, place(j)] = value * jnp.float32(sign) if isinstance(part, int) else value * sign.astype(jnp.float32)
+
+    for unit in range(3):
+        for side in range(2):
+            send_sum(unit, side).wait_send()
+    for unit, part, j in final:
+        hand(unit, part, j).wait()
     for q in range(2):
         for t in range(PIECES):
             for part in range(2):
@@ -233,7 +318,6 @@
     for r in range(2):
         for p in range(naux):
             given_pair(r, p).wait_send()
-    hand().wait()
 
 
 def body(pairs, orbs, match):
@@ -258,17 +342,22 @@
             pltpu.VMEM((2 * nao, nocc), jnp.bfloat16),
             pltpu.VMEM((2 * nao, rounds * combos * 2 * nocc), jnp.bfloat16),
             pltpu.VMEM((nao, 128), jnp.float32),
-            pltpu.VMEM((8, nao), jnp.float32),
             pltpu.VMEM((nao, 128), jnp.float32),
-            pltpu.VMEM((3, 2, 128, nao), jnp.int16),
-            pltpu.VMEM((3, 2, 128, nao), jnp.int16),
+            pltpu.VMEM((3, 4, 128, 128), jnp.int16),
+            pltpu.VMEM((3, 4, 128, 128), jnp.int16),
             pltpu.VMEM((8, nao), jnp.float32),
             pltpu.VMEM((3, 8, nao), jnp.float32),
-            pltpu.VMEM((2, 128, nao), jnp.float32),
-            pltpu.VMEM((2, 64, nao), jnp.float32),
+            pltpu.VMEM((8, nao), jnp.float32),
+            pltpu.VMEM((8, nao), jnp.float32),
+            pltpu.VMEM((3, 128, 128), jnp.float32),
+            pltpu.VMEM((5, 128, 128), jnp.float32),
+            pltpu.VMEM((3, 128, 128), jnp.int16),
+            pltpu.VMEM((2, 3, 64, 128), jnp.int16),
+            pltpu.VMEM((5, 64, 128), jnp.float32),
             dma((rounds, naux)), dma((rounds, naux)), dma((rounds, naux)),
             dma((2, PIECES, 2)), dma((2, PIECES, 2)), dma((2, PIECES)), dma((2, PIECES)),
-            dma((2, 2)), dma((2, 2)), dma((3, 2)), dma((3, 2)), dma((3,)), dma((3,)), dma, dma,
+            dma((2, 2)), dma((2, 2)), dma((3, 4)), dma((3, 4)), dma((3,)), dma((3,)), dma((2,)),
+            dma((3, 2)), dma((2, 3)), dma((5,)), dma((5,)),
         ],
         compiler_params=pltpu.CompilerParams(
             collective_id=0, has_side_effects=True, vmem_limit_bytes=56 << 20

time: 65.8 us -> 57.4 us (0.87)
  Pallas kernels: 63.8 us -> 55.4 us
    pallas_call x1, Pallas kernels: 63.8 us -> 55.4 us  [body(): pl.pallas_call(functools.partial(kernel, factor), out_shape=jax.ShapeDtyp...]
where the time goes in v2:
time: 57.4 us; the launch traced here: 57.3 us
  Pallas kernels  55.4 us (97%)
  local copies, waits for them, and re-layouts  1.87 us (3%)
    pallas_call x1, Pallas kernels, body(): pl.pallas_call(functools.partial(kernel, factor), out_shape=jax.ShapeDtyp...  55.4 us
    unnamed x1, local copies, waits for them, and re-layouts  1.87 us

profile of v2, /device:TPU:1, one launch (start us, length us, event | category | flops | bytes accessed | tf_op | source)
XLA Modules:
  0.0 57.3 jit_solution(17673567473575877062)
XLA Ops:
  0.0 55.4 %shard_map.37 = f32[2,2,64,512]{3,2,1,0:T(8,128)} custom-call(bf16[2,2,2,512,1024]{4,3,2,1,0:T(8,128)(2,1)} %pairs.1, bf16[2,512,512]{2,1,0:T(8,128)(2,1)} %orbs.1, s32[2,64]{1,0:T(2,128)} %match.1), custom_call_target="tpu_custom_call" | custom-call | tf_op jit(solution)/shard_map/pallas_call | solution.py:330
  55.4 1.9 %copy.5 = f32[2,2,64,512]{3,2,1,0:T(8,128)} copy(f32[2,2,64,512]{3,2,1,0:T(8,128)} %shard_map.37) | data formatting | bytes 1048576

commit v3 on v2

--- a/solution.py
+++ b/solution.py
@@ -11,14 +11,18 @@
 ROUNDS = 2
 LEVELS = 32000.0
 SMALLEST = 1e-30
-PIECES = 4
+PIECES = (
+    ((0, 64), (64, 64), (128, 128), (256, 128), (384, 128)),
+    ((0, 128), (128, 128), (256, 128), (384, 64), (448, 64)),
+)
+MOST = 5
 
 
 def kernel(
     factor, pairs, orbs, match, out,
-    held_pairs, c00, c01, c10, c11, block, halves, squares, scale_cols,
+    held_pairs, own_orbs, staged, c00, c01, c10, c11, block, halves, squares, scale_cols,
     codes, codes_in, scales, scales_in, sums_scale, other_scale, turned, total, sums, sums_in, handed,
-    pair_sem, pair_send, pair_recv, x_send, x_recv, relay_send, relay_recv,
+    stage_sem, pair_sem, pair_send, pair_recv, x_send, x_recv, relay_send, relay_recv,
     share_send, share_recv, code_send, code_recv, scale_send, scale_recv, share_scale_sem,
     sum_send, sum_recv, hand_send, hand_recv,
 ):
@@ -27,16 +31,16 @@
     x = kpt // 8
     rest = kpt - x * 8
     near = (x + 1 - 2 * (x % 2)) * 8 + rest
+    far = (x + 2 - 4 * (x // 2)) * 8 + rest
     cross = (3 - x) * 8 + rest
     sibling = aux + 1 - 2 * core
     here = (kpt, sibling)
     nao, nocc = orbs.shape[1], orbs.shape[2] // 2
     width = nocc // 2
-    rows = nao // PIECES
     naux = pairs.shape[2]
     tile = nao // 4
     combos = 2 * naux
-    chosen = ((c00, c01), (c10, c11))
+    far_chunks, near_chunks = (c00, c01), (c10, c11)
 
     def remote(src, dst, send, recv, device):
         return pltpu.make_async_remote_copy(
@@ -54,24 +58,33 @@
             pair_send.at[r, p], pair_recv.at[r, p], here,
         )
 
-    def x_piece(q, t, part):
-        return remote(
-            orbs.at[core, pl.ds(t * rows, rows), pl.ds(part * nocc + q * width, width)],
-            chosen[1][q].at[core, pl.ds(t * rows, rows), pl.ds(part * width, width)],
-            x_send.at[q, t, part], x_recv.at[q, t, part], (near, aux),
+    def stage(k):
+        return pltpu.make_async_copy(orbs.at[k], own_orbs.at[k], stage_sem.at[k])
+
+    def part_of(q, t):
+        return pl.ds(*PIECES[q][t])
+
+    def x_piece(q, t):
+        return remote(
+            staged.at[q, part_of(q, t)], near_chunks[q].at[core, part_of(q, t)],
+            x_send.at[q, t], x_recv.at[q, t], (near, aux),
         )
 
     def relay(q, t):
         return remote(
-            chosen[1][q].at[core, pl.ds(t * rows, rows)], chosen[0][q].at[core, pl.ds(t * rows, rows)],
+            near_chunks[q].at[core, part_of(q, t)], far_chunks[q].at[part_of(q, t)],
             relay_send.at[q, t], relay_recv.at[q, t], (cross, aux),
         )
 
-    def share(r, q):
-        return remote(
-            chosen[r][q].at[core], chosen[r][q].at[core], share_send.at[r, q], share_recv.at[r, q], here
-        )
-
+    def share(q, t):
+        piece = near_chunks[q].at[core, part_of(q, t)]
+        return remote(piece, piece, share_send.at[q, t], share_recv.at[q, t], here)
+
+    def within(r, block, k):
+        return jnp.bitwise_and(match[r, block * 2 + k], 1)
+
+    for k in range(2):
+        stage(k).start()
     for r in (1, 0):
         for p in range(naux):
             own_pair(r, p).start()
@@ -80,78 +93,87 @@
     peers = [(kpt, lax.rem(chip + d, 4) * 2 + side) for d in (1, 2, 3) for side in range(2)]
     for device in [(near, aux), (cross, aux), here] + peers:
         pl.semaphore_signal(barrier, inc=1, device_id=device, device_id_type=MESH)
+    for k in range(2):
+        stage(k).wait()
+    index = within(0, far, core)
+    for q in range(2):
+        for part in range(2):
+            staged[q, :, part * width : (part + 1) * width] = own_orbs[
+                index, :, part * nocc + q * width : part * nocc + (q + 1) * width
+            ]
+
     pl.semaphore_wait(barrier, 9)
 
     for q in range(2):
-        for t in range(PIECES):
-            for part in range(2):
-                x_piece(q, t, part).start()
+        for t in range(MOST):
+            x_piece(q, t).start()
     for r in (1, 0):
         for p in range(naux):
             given_pair(r, p).start()
     squares[...] = jnp.zeros_like(squares)
 
     def pass_on(q, t):
-        for part in range(2):
-            x_piece(q, t, part).wait_recv()
+        x_piece(q, t).wait_recv()
         relay(q, t).start()
+        share(q, t).start()
 
     def build(r, q):
-        index = jnp.bitwise_and(match[r, kpt * 2 + core], 1)
-        both = chosen[r][q][index]
+        if r == 0:
+            both = far_chunks[q][...]
+        else:
+            both = near_chunks[q][jnp.bitwise_xor(within(0, cross, 0), within(1, kpt, core))]
         block[0:nao, :] = both
         block[nao:, 0:width] = -both[:, width:]
         block[nao:, width:] = both[:, 0:width]
 
     def transform(r, q, first, last):
-        def step(p, carry):
+        def step(p):
             done = jnp.dot(held_pairs[r, p], block[...], preferred_element_type=jnp.float32).astype(jnp.bfloat16)
             real, imag = done[:, 0:width], done[:, width:]
-            at = pl.multiple_of((r * combos + p) * 2 * nocc + q * 2 * width, 2 * width)
+            at = (r * combos + p) * 2 * nocc + q * 2 * width
             halves[0:nao, pl.ds(at, 2 * width)] = done
             halves[nao:, pl.ds(at, 2 * width)] = jnp.concatenate([-imag, real], axis=1)
             wide_real, wide_imag = real.astype(jnp.float32), imag.astype(jnp.float32)
             squares[...] += wide_real * wide_real + wide_imag * wide_imag
-            return carry
-
-        lax.fori_loop(first, last, step, 0)
-
-    for t in range(PIECES):
+
+        for p in range(first, last):
+            step(p)
+
+    def pairs_of(r):
+        for p in range(naux):
+            own_pair(r, p).wait()
+        for p in range(naux):
+            given_pair(r, p).wait_recv()
+
+    def near_here(q):
+        for t in range(MOST):
+            share(q, t).wait_recv()
+        build(1, q)
+
+    def far_here(q):
+        for t in range(MOST):
+            relay(q, t).wait_recv()
+        build(0, q)
+
+    for t in range(MOST):
         pass_on(0, t)
-    share(1, 0).start()
-    for p in range(naux):
-        own_pair(1, p).wait()
-    for p in range(naux):
-        given_pair(1, p).wait_recv()
-    share(1, 0).wait_recv()
-    build(1, 0)
-    transform(1, 0, 0, naux)
+    pairs_of(1)
+    near_here(0)
+    transform(1, 0, 0, 1)
     pass_on(1, 0)
-    transform(1, 0, naux, combos)
-    for t in range(PIECES):
-        relay(0, t).wait_recv()
-    share(0, 0).start()
+    transform(1, 0, 1, 4)
     pass_on(1, 1)
-    for p in range(naux):
-        own_pair(0, p).wait()
-    for p in range(naux):
-        given_pair(0, p).wait_recv()
-    share(0, 0).wait_recv()
-    build(0, 0)
-    transform(0, 0, 0, naux)
+    pairs_of(0)
+    far_here(0)
+    transform(0, 0, 0, 3)
     pass_on(1, 2)
-    transform(0, 0, naux, combos)
+    transform(0, 0, 3, 4)
     pass_on(1, 3)
-    share(1, 1).start()
-    share(1, 1).wait_recv()
-    build(1, 1)
-    transform(1, 1, 0, combos)
-    for t in range(PIECES):
-        relay(1, t).wait_recv()
-    share(0, 1).start()
-    share(0, 1).wait_recv()
-    build(0, 1)
-    transform(0, 1, 0, combos)
+    pass_on(1, 4)
+    near_here(1)
+    transform(1, 1, 0, 4)
+    far_here(1)
+    transform(0, 1, 0, 4)
 
     gain = LEVELS ** 0.5
     length = jnp.sqrt(jnp.maximum(jnp.sum(squares[...], axis=1, keepdims=True), SMALLEST))
@@ -203,25 +225,23 @@
             code_send.at[step, unit], code_recv.at[step, unit], peer(step),
         )
 
-    def send_blocks(step, carry):
+    def send_unit(unit, step, carry):
         owner = lax.rem(chip + offset(step), 4)
-        for unit, (j, part) in enumerate(sources(owner)):
+        if unit == 3:
+            j, value = owner, diagonal(owner)
+        else:
+            j, part = sources(owner)[unit]
             value = product(owner, j, part)
-            codes[step, unit] = coded(value.T, scale_cols[place(owner), :], gain / scales[0:1, place(j)])
-            send_codes(step, unit).start()
+        codes[step, unit] = coded(value.T, scale_cols[place(owner), :], gain / scales[0:1, place(j)])
+        send_codes(step, unit).start()
         return carry
 
-    def send_diagonal(step, carry):
-        owner = lax.rem(chip + offset(step), 4)
-        value = diagonal(owner)
-        codes[step, 3] = coded(value.T, scale_cols[place(owner), :], gain / scales[0:1, place(owner)])
-        send_codes(step, 3).start()
-        return carry
-
-    lax.fori_loop(0, 3, send_blocks, 0)
-    for unit, (j, part) in enumerate(sources(chip)):
+    order = (2, 0, 1)
+    for unit in order + (3,):
+        lax.fori_loop(0, 3, functools.partial(send_unit, unit), 0)
+    for unit in order:
+        j, part = sources(chip)[unit]
         total[unit] = product(chip, j, part).T
-    lax.fori_loop(0, 3, send_diagonal, 0)
     total[3] = diagonal(chip).T
 
     summed = scales[...] * scales[...]
@@ -251,7 +271,8 @@
             sums.at[unit, pl.ds(0, 64)], sums_in.at[k, unit], sum_send.at[unit, 0], sum_recv.at[k, unit], here
         )
 
-    for unit, (j, part) in enumerate(sources(chip)):
+    for unit in order:
+        j = sources(chip)[unit][0]
         for step in range(3):
             gather(step, unit, j)
         sums[unit] = coded(
@@ -309,12 +330,10 @@
     for unit, part, j in final:
         hand(unit, part, j).wait()
     for q in range(2):
-        for t in range(PIECES):
-            for part in range(2):
-                x_piece(q, t, part).wait_send()
+        for t in range(MOST):
+            x_piece(q, t).wait_send()
             relay(q, t).wait_send()
-        for r in range(2):
-            share(r, q).wait_send()
+            share(q, t).wait_send()
     for r in range(2):
         for p in range(naux):
             given_pair(r, p).wait_send()
@@ -326,7 +345,8 @@
     factor = 1.0 / (rounds * naux * lax.axis_size("aux") * nocc) ** 0.5
     dma = pltpu.SemaphoreType.DMA
     combos = 2 * naux
-    orbital_chunk = pltpu.VMEM((per_device, nao, nocc), jnp.bfloat16)
+    far_chunk = pltpu.VMEM((nao, nocc), jnp.bfloat16)
+    near_chunk = pltpu.VMEM((per_device, nao, nocc), jnp.bfloat16)
     return pl.pallas_call(
         functools.partial(kernel, factor),
         out_shape=jax.ShapeDtypeStruct((per_device, 2, nao // 8, nao), jnp.float32),
@@ -338,7 +358,9 @@
         out_specs=pl.BlockSpec(memory_space=pltpu.VMEM),
         scratch_shapes=[
             pltpu.VMEM((rounds, combos, nao, 2 * nao), jnp.bfloat16),
-            orbital_chunk, orbital_chunk, orbital_chunk, orbital_chunk,
+            pltpu.VMEM((per_device, nao, 2 * nocc), jnp.bfloat16),
+            pltpu.VMEM((2, nao, nocc), jnp.bfloat16),
+            far_chunk, far_chunk, near_chunk, near_chunk,
             pltpu.VMEM((2 * nao, nocc), jnp.bfloat16),
             pltpu.VMEM((2 * nao, rounds * combos * 2 * nocc), jnp.bfloat16),
             pltpu.VMEM((nao, 128), jnp.float32),
@@ -354,9 +376,9 @@
             pltpu.VMEM((3, 128, 128), jnp.int16),
             pltpu.VMEM((2, 3, 64, 128), jnp.int16),
             pltpu.VMEM((5, 64, 128), jnp.float32),
-            dma((rounds, naux)), dma((rounds, naux)), dma((rounds, naux)),
-            dma((2, PIECES, 2)), dma((2, PIECES, 2)), dma((2, PIECES)), dma((2, PIECES)),
-            dma((2, 2)), dma((2, 2)), dma((3, 4)), dma((3, 4)), dma((3,)), dma((3,)), dma((2,)),
+            dma((per_device,)), dma((rounds, naux)), dma((rounds, naux)), dma((rounds, naux)),
+            dma((2, MOST)), dma((2, MOST)), dma((2, MOST)), dma((2, MOST)),
+            dma((2, MOST)), dma((2, MOST)), dma((3, 4)), dma((3, 4)), dma((3,)), dma((3,)), dma((2,)),
             dma((3, 2)), dma((2, 3)), dma((5,)), dma((5,)),
         ],
         compiler_params=pltpu.CompilerParams(

time: 57.4 us -> 52.6 us (0.916)
  Pallas kernels: 55.4 us -> 50.5 us
    pallas_call x1, Pallas kernels: 55.4 us -> 50.5 us  [body(): pl.pallas_call(functools.partial(kernel, factor), out_shape=jax.ShapeDtyp...]
where the time goes in v3:
time: 52.6 us; the launch traced here: 52.4 us
  Pallas kernels  50.5 us (96%)
  local copies, waits for them, and re-layouts  1.87 us (4%)
    pallas_call x1, Pallas kernels, body(): pl.pallas_call(functools.partial(kernel, factor), out_shape=jax.ShapeDtyp...  50.5 us
    unnamed x1, local copies, waits for them, and re-layouts  1.87 us

profile of v3, /device:TPU:1, one launch (start us, length us, event | category | flops | bytes accessed | tf_op | source)
XLA Modules:
  0.0 52.4 jit_solution(15582317208826379627)
XLA Ops:
  0.0 50.5 %shard_map.37 = f32[2,2,64,512]{3,2,1,0:T(8,128)} custom-call(bf16[2,2,2,512,1024]{4,3,2,1,0:T(8,128)(2,1)} %pairs.1, bf16[2,512,512]{2,1,0:T(8,128)(2,1)} %orbs.1, s32[2,64]{1,0:T(2,128)} %match.1), custom_call_target="tpu_custom_call" | custom-call | tf_op jit(solution)/shard_map/pallas_call | solution.py:350
  50.5 1.9 %copy.5 = f32[2,2,64,512]{3,2,1,0:T(8,128)} copy(f32[2,2,64,512]{3,2,1,0:T(8,128)} %shard_map.37) | data formatting | bytes 1048576

commit v4 on v3

--- a/solution.py
+++ b/solution.py
@@ -19,8 +19,8 @@
 
 
 def kernel(
-    factor, pairs, orbs, match, out,
-    held_pairs, own_orbs, staged, c00, c01, c10, c11, block, halves, squares, scale_cols,
+    factor, pairs, orbs, match_far, out,
+    match, match_sem, held_pairs, own_orbs, staged, c00, c01, c10, c11, block, halves, squares, scale_cols,
     codes, codes_in, scales, scales_in, sums_scale, other_scale, turned, total, sums, sums_in, handed,
     stage_sem, pair_sem, pair_send, pair_recv, x_send, x_recv, relay_send, relay_recv,
     share_send, share_recv, code_send, code_recv, scale_send, scale_recv, share_scale_sem,
@@ -83,6 +83,8 @@
     def within(r, block, k):
         return jnp.bitwise_and(match[r, block * 2 + k], 1)
 
+    indices = pltpu.make_async_copy(match_far, match, match_sem)
+    indices.start()
     for k in range(2):
         stage(k).start()
     for r in (1, 0):
@@ -95,6 +97,7 @@
         pl.semaphore_signal(barrier, inc=1, device_id=device, device_id_type=MESH)
     for k in range(2):
         stage(k).wait()
+    indices.wait()
     index = within(0, far, core)
     for q in range(2):
         for part in range(2):
@@ -353,10 +356,11 @@
         in_specs=[
             pl.BlockSpec(memory_space=pl.ANY),
             pl.BlockSpec(memory_space=pl.ANY),
-            pl.BlockSpec(memory_space=pltpu.SMEM),
+            pl.BlockSpec(memory_space=pl.ANY),
         ],
         out_specs=pl.BlockSpec(memory_space=pltpu.VMEM),
         scratch_shapes=[
+            pltpu.SMEM((2, 64), jnp.int32), dma,
             pltpu.VMEM((rounds, combos, nao, 2 * nao), jnp.bfloat16),
             pltpu.VMEM((per_device, nao, 2 * nocc), jnp.bfloat16),
             pltpu.VMEM((2, nao, nocc), jnp.bfloat16),
@@ -382,7 +386,7 @@
             dma((3, 2)), dma((2, 3)), dma((5,)), dma((5,)),
         ],
         compiler_params=pltpu.CompilerParams(
-            collective_id=0, has_side_effects=True, vmem_limit_bytes=56 << 20
+            collective_id=0, has_side_effects=True, vmem_limit_bytes=53 << 20
         ),
     )(pairs, orbs, match)
 

time: 52.6 us -> 50.4 us (0.958)
  Pallas kernels: 50.5 us -> 48.7 us
    pallas_call x1, Pallas kernels: 50.5 us -> 48.7 us  [body(): pl.pallas_call(functools.partial(kernel, factor), out_shape=jax.ShapeDtyp...]
    unnamed x1 -> x3, local copies, waits for them, and re-layouts: 1.87 us -> 1.47 us
where the time goes in v4:
time: 50.4 us; the launch traced here: 50.2 us
  Pallas kernels  48.7 us (97%)
  local copies, waits for them, and re-layouts  1.47 us (3%)
    pallas_call x1, Pallas kernels, body(): pl.pallas_call(functools.partial(kernel, factor), out_shape=jax.ShapeDtyp...  48.7 us
    unnamed x3, local copies, waits for them, and re-layouts  1.47 us

profile of v4, /device:TPU:1, one launch (start us, length us, event | category | flops | bytes accessed | tf_op | source)
XLA Modules:
  0.0 50.2 jit_solution(10202642612012160641)
XLA Ops:
  0.0 0.0 copy-start
  0.0 0.7 %copy-done = s32[2,64]{1,0:T(2,128)S(1)} copy-done((s32[2,64]{1,0:T(2,128)S(1)}, s32[2,64]{1,0:T(2,128)}, u32[]{:S(2)}) %copy-start) | copy-done | bytes 536
  0.7 48.7 %shard_map.37 = f32[2,2,64,512]{3,2,1,0:T(8,128)S(1)} custom-call(bf16[2,2,2,512,1024]{4,3,2,1,0:T(8,128)(2,1)} %pairs.1, bf16[2,512,512]{2,1,0:T(8,128)(2,1)} %orbs.1, s32[2,64]{1,0:T(2,128)S(1)} %copy-done), custom_call_target="tpu_custom_call" | custom-call | tf_op jit(solution)/shard_map/pallas_call | solution.py:353
  49.4 0.8 %copy.5 = f32[2,2,64,512]{3,2,1,0:T(8,128)} copy(f32[2,2,64,512]{3,2,1,0:T(8,128)S(1)} %shard_map.37) | data formatting | bytes 1048576
Async XLA Ops:
  0.0 0.7 %copy-start = (s32[2,64]{1,0:T(2,128)S(1)}, s32[2,64]{1,0:T(2,128)}, u32[]{:S(2)}) copy-start(s32[2,64]{1,0:T(2,128)} %match_far.1) | copy-start | bytes 1540

commit v5 on v4

--- a/solution.py
+++ b/solution.py
@@ -13,7 +13,7 @@
 SMALLEST = 1e-30
 PIECES = (
     ((0, 64), (64, 64), (128, 128), (256, 128), (384, 128)),
-    ((0, 128), (128, 128), (256, 128), (384, 64), (448, 64)),
+    ((0, 32), (128, 128), (256, 128), (384, 64), (448, 64)),
 )
 MOST = 5
 
@@ -22,7 +22,7 @@
     factor, pairs, orbs, match_far, out,
     match, match_sem, held_pairs, own_orbs, staged, c00, c01, c10, c11, block, halves, squares, scale_cols,
     codes, codes_in, scales, scales_in, sums_scale, other_scale, turned, total, sums, sums_in, handed,
-    stage_sem, pair_sem, pair_send, pair_recv, x_send, x_recv, relay_send, relay_recv,
+    stage_sem, pair_sem, pair_send, pair_recv, x_send, x_recv, relay_send, relay_recv, quarter_send, quarter_recv,
     share_send, share_recv, code_send, code_recv, scale_send, scale_recv, share_scale_sem,
     sum_send, sum_recv, hand_send, hand_recv,
 ):
@@ -62,7 +62,21 @@
         return pltpu.make_async_copy(orbs.at[k], own_orbs.at[k], stage_sem.at[k])
 
     def part_of(q, t):
-        return pl.ds(*PIECES[q][t])
+        start, size = PIECES[q][t]
+        if (q, t) == (1, 0):
+            return pl.ds(pl.multiple_of(chip * size, size), size)
+        return pl.ds(start, size)
+
+    def spread_out(r, d):
+        piece = (near_chunks[1].at[core] if r else far_chunks[1]).at[part_of(1, 0)]
+        return remote(
+            piece, piece, quarter_send.at[r, d - 1], quarter_recv.at[r, d - 1],
+            (kpt, lax.rem(chip + d, 4) * 2 + core),
+        )
+
+    def whole_share():
+        piece = near_chunks[1].at[core, pl.ds(0, 128)]
+        return remote(piece, piece, share_send.at[1, 0], share_recv.at[1, 0], here)
 
     def x_piece(q, t):
         return remote(
@@ -107,9 +121,11 @@
 
     pl.semaphore_wait(barrier, 9)
 
+    x_piece(1, 0).start()
     for q in range(2):
         for t in range(MOST):
-            x_piece(q, t).start()
+            if (q, t) != (1, 0):
+                x_piece(q, t).start()
     for r in (1, 0):
         for p in range(naux):
             given_pair(r, p).start()
@@ -118,7 +134,21 @@
     def pass_on(q, t):
         x_piece(q, t).wait_recv()
         relay(q, t).start()
-        share(q, t).start()
+        if (q, t) == (1, 0):
+            for d in (2, 1, 3):
+                spread_out(1, d).start()
+        else:
+            share(q, t).start()
+
+    def spread_far():
+        relay(1, 0).wait_recv()
+        for d in (2, 1, 3):
+            spread_out(0, d).start()
+
+    def near_quarters():
+        for d in (1, 2, 3):
+            spread_out(1, d).wait_recv()
+        whole_share().start()
 
     def build(r, q):
         if r == 0:
@@ -150,28 +180,39 @@
 
     def near_here(q):
         for t in range(MOST):
-            share(q, t).wait_recv()
+            if (q, t) == (1, 0):
+                whole_share().wait_recv()
+            else:
+                share(q, t).wait_recv()
         build(1, q)
 
     def far_here(q):
         for t in range(MOST):
-            relay(q, t).wait_recv()
+            if (q, t) != (1, 0):
+                relay(q, t).wait_recv()
+        if q == 1:
+            for d in (1, 2, 3):
+                spread_out(0, d).wait_recv()
         build(0, q)
 
-    for t in range(MOST):
+    pass_on(1, 0)
+    pass_on(0, 0)
+    pass_on(0, 1)
+    spread_far()
+    for t in range(2, MOST):
         pass_on(0, t)
     pairs_of(1)
     near_here(0)
     transform(1, 0, 0, 1)
-    pass_on(1, 0)
+    pass_on(1, 1)
     transform(1, 0, 1, 4)
-    pass_on(1, 1)
+    pass_on(1, 2)
     pairs_of(0)
     far_here(0)
-    transform(0, 0, 0, 3)
-    pass_on(1, 2)
-    transform(0, 0, 3, 4)
+    transform(0, 0, 0, 2)
     pass_on(1, 3)
+    near_quarters()
+    transform(0, 0, 2, 4)
     pass_on(1, 4)
     near_here(1)
     transform(1, 1, 0, 4)
@@ -240,12 +281,15 @@
         return carry
 
     order = (2, 0, 1)
-    for unit in order + (3,):
+    for unit in order:
         lax.fori_loop(0, 3, functools.partial(send_unit, unit), 0)
-    for unit in order:
+
+    def own(unit):
         j, part = sources(chip)[unit]
         total[unit] = product(chip, j, part).T
-    total[3] = diagonal(chip).T
+
+    own(order[0])
+    lax.fori_loop(0, 3, functools.partial(send_unit, 3), 0)
 
     summed = scales[...] * scales[...]
     for step in range(3):
@@ -276,6 +320,8 @@
 
     for unit in order:
         j = sources(chip)[unit][0]
+        if unit != order[0]:
+            own(unit)
         for step in range(3):
             gather(step, unit, j)
         sums[unit] = coded(
@@ -283,6 +329,8 @@
         )
         for side in range(2):
             send_sum(unit, side).start()
+
+    total[3] = diagonal(chip).T
 
     def hand(unit, part, j):
         return remote(
@@ -336,8 +384,12 @@
         for t in range(MOST):
             x_piece(q, t).wait_send()
             relay(q, t).wait_send()
-            share(q, t).wait_send()
+            if (q, t) != (1, 0):
+                share(q, t).wait_send()
+    whole_share().wait_send()
     for r in range(2):
+        for d in (1, 2, 3):
+            spread_out(r, d).wait_send()
         for p in range(naux):
             given_pair(r, p).wait_send()
 
@@ -382,7 +434,7 @@
             pltpu.VMEM((5, 64, 128), jnp.float32),
             dma((per_device,)), dma((rounds, naux)), dma((rounds, naux)), dma((rounds, naux)),
             dma((2, MOST)), dma((2, MOST)), dma((2, MOST)), dma((2, MOST)),
-            dma((2, MOST)), dma((2, MOST)), dma((3, 4)), dma((3, 4)), dma((3,)), dma((3,)), dma((2,)),
+            dma((2, 3)), dma((2, 3)), dma((2, MOST)), dma((2, MOST)), dma((3, 4)), dma((3, 4)), dma((3,)), dma((3,)), dma((2,)),
             dma((3, 2)), dma((2, 3)), dma((5,)), dma((5,)),
         ],
         compiler_params=pltpu.CompilerParams(

time: 50.4 us -> 49.2 us (0.976)
  Pallas kernels: 48.7 us -> 47.6 us
    pallas_call x1, Pallas kernels: 48.7 us -> 47.6 us  [body(): pl.pallas_call(functools.partial(kernel, factor), out_shape=jax.ShapeDtyp...]
where the time goes in v5:
time: 49.2 us; the launch traced here: 49.1 us
  Pallas kernels  47.6 us (97%)
  local copies, waits for them, and re-layouts  1.47 us (3%)
    pallas_call x1, Pallas kernels, body(): pl.pallas_call(functools.partial(kernel, factor), out_shape=jax.ShapeDtyp...  47.6 us
    unnamed x3, local copies, waits for them, and re-layouts  1.47 us

profile of v5, /device:TPU:1, one launch (start us, length us, event | category | flops | bytes accessed | tf_op | source)
XLA Modules:
  0.0 49.1 jit_solution(13210107302516452420)
XLA Ops:
  0.0 0.0 copy-start
  0.0 0.7 %copy-done = s32[2,64]{1,0:T(2,128)S(1)} copy-done((s32[2,64]{1,0:T(2,128)S(1)}, s32[2,64]{1,0:T(2,128)}, u32[]{:S(2)}) %copy-start) | copy-done | bytes 536
  0.7 47.6 %shard_map.37 = f32[2,2,64,512]{3,2,1,0:T(8,128)S(1)} custom-call(bf16[2,2,2,512,1024]{4,3,2,1,0:T(8,128)(2,1)} %pairs.1, bf16[2,512,512]{2,1,0:T(8,128)(2,1)} %orbs.1, s32[2,64]{1,0:T(2,128)S(1)} %copy-done), custom_call_target="tpu_custom_call" | custom-call | tf_op jit(solution)/shard_map/pallas_call | solution.py:405
  48.3 0.8 %copy.5 = f32[2,2,64,512]{3,2,1,0:T(8,128)} copy(f32[2,2,64,512]{3,2,1,0:T(8,128)S(1)} %shard_map.37) | data formatting | bytes 1048576
Async XLA Ops:
  0.0 0.7 %copy-start = (s32[2,64]{1,0:T(2,128)S(1)}, s32[2,64]{1,0:T(2,128)}, u32[]{:S(2)}) copy-start(s32[2,64]{1,0:T(2,128)} %match_far.1) | copy-start | bytes 1540

commit v6 on v5

--- a/solution.py
+++ b/solution.py
@@ -21,9 +21,9 @@
 def kernel(
     factor, pairs, orbs, match_far, out,
     match, match_sem, held_pairs, own_orbs, staged, c00, c01, c10, c11, block, halves, squares, scale_cols,
-    codes, codes_in, scales, scales_in, sums_scale, other_scale, turned, total, sums, sums_in, handed,
+    far_codes, far_in, codes, codes_in, passed_scale, joined_scale, scales, scales_in, sums_scale, other_scale, turned, total, sums, sums_in, handed,
     stage_sem, pair_sem, pair_send, pair_recv, x_send, x_recv, relay_send, relay_recv, quarter_send, quarter_recv,
-    share_send, share_recv, code_send, code_recv, scale_send, scale_recv, share_scale_sem,
+    share_send, share_recv, far_send, far_recv, code_send, code_recv, scale_send, scale_recv, share_scale_sem,
     sum_send, sum_recv, hand_send, hand_recv,
 ):
     kpt, aux = lax.axis_index("kpt"), lax.axis_index("aux")
@@ -263,48 +263,83 @@
     def coded(value, rows_scale, cols_scale):
         return jnp.round(value * rows_scale * cols_scale).astype(jnp.int32).astype(jnp.int16)
 
-    def send_codes(step, unit):
-        return remote(
-            codes.at[step, unit], codes_in.at[step, unit],
-            code_send.at[step, unit], code_recv.at[step, unit], peer(step),
-        )
-
-    def send_unit(unit, step, carry):
-        owner = lax.rem(chip + offset(step), 4)
+    order = (2, 1, 0)
+    ways = (1, 3, 1, 3)
+
+    def chip_at(distance):
+        return lax.rem(chip + distance, 4)
+
+    def column(scale, block):
+        return jnp.broadcast_to(scale[0:1, place(block)], (tile, tile)).T
+
+    def contribution(unit, owner):
         if unit == 3:
-            j, value = owner, diagonal(owner)
-        else:
-            j, part = sources(owner)[unit]
-            value = product(owner, j, part)
-        codes[step, unit] = coded(value.T, scale_cols[place(owner), :], gain / scales[0:1, place(j)])
-        send_codes(step, unit).start()
-        return carry
-
-    order = (2, 0, 1)
-    for unit in order:
-        lax.fori_loop(0, 3, functools.partial(send_unit, unit), 0)
-
-    def own(unit):
-        j, part = sources(chip)[unit]
-        total[unit] = product(chip, j, part).T
-
-    own(order[0])
-    lax.fori_loop(0, 3, functools.partial(send_unit, 3), 0)
-
-    summed = scales[...] * scales[...]
+            return owner, diagonal(owner).T
+        j, part = sources(owner)[unit]
+        return j, product(owner, j, part).T
+
+    def send_far(unit):
+        return remote(
+            far_codes.at[unit], far_in.at[unit], far_send.at[unit], far_recv.at[unit],
+            (kpt, chip_at(ways[unit]) * 2 + core),
+        )
+
+    def send_codes(joined, unit):
+        distance = ways[unit] if joined else 4 - ways[unit]
+        return remote(
+            codes.at[joined, unit], codes_in.at[joined, unit],
+            code_send.at[joined, unit], code_recv.at[joined, unit], (kpt, chip_at(distance) * 2 + core),
+        )
+
+    def coded_alone(unit, owner):
+        j, value = contribution(unit, owner)
+        return coded(value, scale_cols[place(owner), :], gain / scales[0:1, place(j)])
+
+    for unit in order + (3,):
+        far_codes[unit] = coded_alone(unit, chip_at(2))
+        send_far(unit).start()
+    for unit in order + (3,):
+        codes[0, unit] = coded_alone(unit, chip_at(4 - ways[unit]))
+        send_codes(0, unit).start()
+
+    own_squares = scales[...] * scales[...]
+    summed = own_squares
     for step in range(3):
         send_scales(step).wait()
         summed += scales_in[step] * scales_in[step]
-        received = scales_in[step, 0:1, place(chip)]
-        turned[step] = jnp.broadcast_to(received, (tile, tile)).T * (1.0 / LEVELS)
     sums_scale[...] = jnp.sqrt(summed)
     share_scales().start()
-    own_turned = jnp.broadcast_to(sums_scale[0:1, place(chip)], (tile, tile)).T
-
-    def gather(step, unit, j):
-        send_codes(step, unit).wait()
-        wide = codes_in[step, unit].astype(jnp.int32).astype(jnp.float32)
-        total[unit] += wide * turned[step] * scales_in[step, 0:1, place(j)]
+    for way, step in ((0, 1), (1, 2)):
+        one = scales_in[step] * scales_in[step]
+        passed_scale[way] = jnp.sqrt(own_squares + one)
+        joined_scale[way] = jnp.sqrt(one + scales_in[0] * scales_in[0])
+        ahead = chip_at(1 + 2 * way)
+        turned[way] = column(scales_in.at[step], ahead) * (1.0 / LEVELS)
+        turned[2 + way] = gain / column(passed_scale.at[way], ahead)
+
+    for unit in order + (3,):
+        way = ways[unit] // 2
+        j, value = contribution(unit, chip_at(ways[unit]))
+        send_far(unit).wait()
+        before = far_in[unit].astype(jnp.int32).astype(jnp.float32)
+        value += before * turned[way] * scales_in[1 + way, 0:1, place(j)]
+        codes[1, unit] = coded(value, turned[2 + way], gain / passed_scale[way, 0:1, place(j)])
+        send_codes(1, unit).start()
+
+    for way in range(2):
+        turned[way] = column(scales_in.at[2 - way], chip) * (1.0 / LEVELS)
+        turned[2 + way] = column(joined_scale.at[way], chip) * (1.0 / LEVELS)
+    own_turned = column(sums_scale, chip)
+
+    def gather(unit):
+        way = ways[unit] // 2
+        j, value = contribution(unit, chip)
+        send_codes(0, unit).wait()
+        wide = codes_in[0, unit].astype(jnp.int32).astype(jnp.float32)
+        value += wide * turned[way] * scales_in[2 - way, 0:1, place(j)]
+        send_codes(1, unit).wait()
+        wide = codes_in[1, unit].astype(jnp.int32).astype(jnp.float32)
+        total[unit] = value + wide * turned[2 + way] * joined_scale[way, 0:1, place(j)]
 
     def send_sum(unit, side):
         j = sources(chip)[unit][0]
@@ -320,17 +355,12 @@
 
     for unit in order:
         j = sources(chip)[unit][0]
-        if unit != order[0]:
-            own(unit)
-        for step in range(3):
-            gather(step, unit, j)
+        gather(unit)
         sums[unit] = coded(
             (total[unit] * (gain / own_turned) * (gain / sums_scale[0:1, place(j)])).T, 1.0, 1.0
         )
         for side in range(2):
             send_sum(unit, side).start()
-
-    total[3] = diagonal(chip).T
 
     def hand(unit, part, j):
         return remote(
@@ -345,8 +375,7 @@
         handed[unit] = total[unit, theirs, :] * factor
         hand(unit, part, j).start()
         out[core, part, :, place(j)] = total[unit, mine, :] * factor
-    for step in range(3):
-        gather(step, 3, chip)
+    gather(3)
     packed = total[3] * factor
     turned[0] = packed.T
     strict = lax.broadcasted_iota(jnp.int32, (tile, tile), 0) > lax.broadcasted_iota(jnp.int32, (tile, tile), 1)
@@ -421,20 +450,24 @@
             pltpu.VMEM((2 * nao, rounds * combos * 2 * nocc), jnp.bfloat16),
             pltpu.VMEM((nao, 128), jnp.float32),
             pltpu.VMEM((nao, 128), jnp.float32),
-            pltpu.VMEM((3, 4, 128, 128), jnp.int16),
-            pltpu.VMEM((3, 4, 128, 128), jnp.int16),
+            pltpu.VMEM((4, 128, 128), jnp.int16),
+            pltpu.VMEM((4, 128, 128), jnp.int16),
+            pltpu.VMEM((2, 4, 128, 128), jnp.int16),
+            pltpu.VMEM((2, 4, 128, 128), jnp.int16),
+            pltpu.VMEM((2, 8, nao), jnp.float32),
+            pltpu.VMEM((2, 8, nao), jnp.float32),
             pltpu.VMEM((8, nao), jnp.float32),
             pltpu.VMEM((3, 8, nao), jnp.float32),
             pltpu.VMEM((8, nao), jnp.float32),
             pltpu.VMEM((8, nao), jnp.float32),
-            pltpu.VMEM((3, 128, 128), jnp.float32),
+            pltpu.VMEM((4, 128, 128), jnp.float32),
             pltpu.VMEM((5, 128, 128), jnp.float32),
             pltpu.VMEM((3, 128, 128), jnp.int16),
             pltpu.VMEM((2, 3, 64, 128), jnp.int16),
             pltpu.VMEM((5, 64, 128), jnp.float32),
             dma((per_device,)), dma((rounds, naux)), dma((rounds, naux)), dma((rounds, naux)),
             dma((2, MOST)), dma((2, MOST)), dma((2, MOST)), dma((2, MOST)),
-            dma((2, 3)), dma((2, 3)), dma((2, MOST)), dma((2, MOST)), dma((3, 4)), dma((3, 4)), dma((3,)), dma((3,)), dma((2,)),
+            dma((2, 3)), dma((2, 3)), dma((2, MOST)), dma((2, MOST)), dma((4,)), dma((4,)), dma((2, 4)), dma((2, 4)), dma((3,)), dma((3,)), dma((2,)),
             dma((3, 2)), dma((2, 3)), dma((5,)), dma((5,)),
         ],
         compiler_params=pltpu.CompilerParams(

time: 49.2 us -> 48.4 us (0.984)
  Pallas kernels: 47.6 us -> 46.9 us
    pallas_call x1, Pallas kernels: 47.6 us -> 46.9 us  [body(): pl.pallas_call(functools.partial(kernel, factor), out_shape=jax.ShapeDtyp...]
where the time goes in v6:
time: 48.4 us; the launch traced here: 48.3 us
  Pallas kernels  46.9 us (97%)
  local copies, waits for them, and re-layouts  1.47 us (3%)
    pallas_call x1, Pallas kernels, body(): pl.pallas_call(functools.partial(kernel, factor), out_shape=jax.ShapeDtyp...  46.9 us
    unnamed x3, local copies, waits for them, and re-layouts  1.47 us

profile of v6, /device:TPU:1, one launch (start us, length us, event | category | flops | bytes accessed | tf_op | source)
XLA Modules:
  0.0 48.3 jit_solution(15588779876265652217)
XLA Ops:
  0.0 0.0 copy-start
  0.0 0.7 %copy-done = s32[2,64]{1,0:T(2,128)S(1)} copy-done((s32[2,64]{1,0:T(2,128)S(1)}, s32[2,64]{1,0:T(2,128)}, u32[]{:S(2)}) %copy-start) | copy-done | bytes 536
  0.7 46.9 %shard_map.37 = f32[2,2,64,512]{3,2,1,0:T(8,128)S(1)} custom-call(bf16[2,2,2,512,1024]{4,3,2,1,0:T(8,128)(2,1)} %pairs.1, bf16[2,512,512]{2,1,0:T(8,128)(2,1)} %orbs.1, s32[2,64]{1,0:T(2,128)S(1)} %copy-done), custom_call_target="tpu_custom_call" | custom-call | tf_op jit(solution)/shard_map/pallas_call | solution.py:434
  47.6 0.8 %copy.5 = f32[2,2,64,512]{3,2,1,0:T(8,128)} copy(f32[2,2,64,512]{3,2,1,0:T(8,128)S(1)} %shard_map.37) | data formatting | bytes 1048576
Async XLA Ops:
  0.0 0.7 %copy-start = (s32[2,64]{1,0:T(2,128)S(1)}, s32[2,64]{1,0:T(2,128)}, u32[]{:S(2)}) copy-start(s32[2,64]{1,0:T(2,128)} %match_far.1) | copy-start | bytes 1540

commit v7 on v6

--- a/solution.py
+++ b/solution.py
@@ -473,7 +473,7 @@
         compiler_params=pltpu.CompilerParams(
             collective_id=0, has_side_effects=True, vmem_limit_bytes=53 << 20
         ),
-    )(pairs, orbs, match)
+    )(pairs, orbs, pltpu.with_memory_space_constraint(match, pltpu.HBM))
 
 
 def solution(mesh):

time: 48.4 us -> 47.8 us (0.988)
  local copies, waits for them, and re-layouts: 1.47 us -> 0.8 us
    unnamed x3 -> x1, local copies, waits for them, and re-layouts: 1.47 us -> 0.8 us
where the time goes in v7:
time: 47.8 us; the launch traced here: 47.7 us
  Pallas kernels  46.9 us (98%)
  local copies, waits for them, and re-layouts  0.8 us (2%)
    pallas_call x1, Pallas kernels, body(): pl.pallas_call(functools.partial(kernel, factor), out_shape=jax.ShapeDtyp...  46.9 us

profile of v7, /device:TPU:1, one launch (start us, length us, event | category | flops | bytes accessed | tf_op | source)
XLA Modules:
  0.0 47.7 jit_solution(15353661807783486414)
XLA Ops:
  0.0 46.9 %shard_map.37 = f32[2,2,64,512]{3,2,1,0:T(8,128)S(1)} custom-call(bf16[2,2,2,512,1024]{4,3,2,1,0:T(8,128)(2,1)} %pairs.1, bf16[2,512,512]{2,1,0:T(8,128)(2,1)} %orbs.1, s32[2,64]{1,0:T(2,128)} %match_far.1), custom_call_target="tpu_custom_call" | custom-call | tf_op jit(solution)/shard_map/pallas_call | solution.py:434
  46.9 0.8 %copy.5 = f32[2,2,64,512]{3,2,1,0:T(8,128)} copy(f32[2,2,64,512]{3,2,1,0:T(8,128)S(1)} %shard_map.37) | data formatting | bytes 1048576

commit v8 on v7

--- a/solution.py
+++ b/solution.py
@@ -97,18 +97,14 @@
     def within(r, block, k):
         return jnp.bitwise_and(match[r, block * 2 + k], 1)
 
+    barrier = pltpu.get_barrier_semaphore()
+    peers = [(kpt, lax.rem(chip + d, 4) * 2 + side) for d in (1, 2, 3) for side in range(2)]
+    for device in [(near, aux), (cross, aux), here] + peers:
+        pl.semaphore_signal(barrier, inc=1, device_id=device, device_id_type=MESH)
     indices = pltpu.make_async_copy(match_far, match, match_sem)
     indices.start()
     for k in range(2):
         stage(k).start()
-    for r in (1, 0):
-        for p in range(naux):
-            own_pair(r, p).start()
-
-    barrier = pltpu.get_barrier_semaphore()
-    peers = [(kpt, lax.rem(chip + d, 4) * 2 + side) for d in (1, 2, 3) for side in range(2)]
-    for device in [(near, aux), (cross, aux), here] + peers:
-        pl.semaphore_signal(barrier, inc=1, device_id=device, device_id_type=MESH)
     for k in range(2):
         stage(k).wait()
     indices.wait()
@@ -128,6 +124,7 @@
                 x_piece(q, t).start()
     for r in (1, 0):
         for p in range(naux):
+            own_pair(r, p).start()
             given_pair(r, p).start()
     squares[...] = jnp.zeros_like(squares)
 
@@ -305,7 +302,7 @@
     own_squares = scales[...] * scales[...]
     summed = own_squares
     for step in range(3):
-        send_scales(step).wait()
+        send_scales(step).wait_recv()
         summed += scales_in[step] * scales_in[step]
     sums_scale[...] = jnp.sqrt(summed)
     share_scales().start()
@@ -320,7 +317,7 @@
     for unit in order + (3,):
         way = ways[unit] // 2
         j, value = contribution(unit, chip_at(ways[unit]))
-        send_far(unit).wait()
+        send_far(unit).wait_recv()
         before = far_in[unit].astype(jnp.int32).astype(jnp.float32)
         value += before * turned[way] * scales_in[1 + way, 0:1, place(j)]
         codes[1, unit] = coded(value, turned[2 + way], gain / passed_scale[way, 0:1, place(j)])
@@ -334,10 +331,10 @@
     def gather(unit):
         way = ways[unit] // 2
         j, value = contribution(unit, chip)
-        send_codes(0, unit).wait()
+        send_codes(0, unit).wait_recv()
         wide = codes_in[0, unit].astype(jnp.int32).astype(jnp.float32)
         value += wide * turned[way] * scales_in[2 - way, 0:1, place(j)]
-        send_codes(1, unit).wait()
+        send_codes(1, unit).wait_recv()
         wide = codes_in[1, unit].astype(jnp.int32).astype(jnp.float32)
         total[unit] = value + wide * turned[2 + way] * joined_scale[way, 0:1, place(j)]
 
@@ -388,7 +385,7 @@
         hand(unit, part, j).start()
         out[core, part, :, place(j)] = total[unit, mine, :]
 
-    share_scales().wait()
+    share_scales().wait_recv()
     for same in range(2):
         k = core if same == 1 else 1 - core
         scale = sums_scale if same == 1 else other_scale
@@ -404,6 +401,13 @@
             value = wide * down * scale[0:1, place(j)]
             out[k, part, :, place(j)] = value * jnp.float32(sign) if isinstance(part, int) else value * sign.astype(jnp.float32)
 
+    share_scales().wait_send()
+    for step in range(3):
+        send_scales(step).wait_send()
+    for unit in range(4):
+        send_far(unit).wait_send()
+        for joint in range(2):
+            send_codes(joint, unit).wait_send()
     for unit in range(3):
         for side in range(2):
             send_sum(unit, side).wait_send()

time: 47.8 us -> 48 us (level)
  no operation moved by 1% of the time
where the time goes in v8:
time: 48 us; the launch traced here: 47.9 us
  Pallas kernels  47.1 us (98%)
  local copies, waits for them, and re-layouts  0.8 us (2%)
    pallas_call x1, Pallas kernels, body(): pl.pallas_call(functools.partial(kernel, factor), out_shape=jax.ShapeDtyp...  47.1 us

profile of v8, /device:TPU:1, one launch (start us, length us, event | category | flops | bytes accessed | tf_op | source)
XLA Modules:
  0.0 47.9 jit_solution(4344853437768023585)
XLA Ops:
  0.0 47.1 %shard_map.37 = f32[2,2,64,512]{3,2,1,0:T(8,128)S(1)} custom-call(bf16[2,2,2,512,1024]{4,3,2,1,0:T(8,128)(2,1)} %pairs.1, bf16[2,512,512]{2,1,0:T(8,128)(2,1)} %orbs.1, s32[2,64]{1,0:T(2,128)} %match_far.1), custom_call_target="tpu_custom_call" | custom-call | tf_op jit(solution)/shard_map/pallas_call | solution.py:438
  47.1 0.8 %copy.5 = f32[2,2,64,512]{3,2,1,0:T(8,128)} copy(f32[2,2,64,512]{3,2,1,0:T(8,128)S(1)} %shard_map.37) | data formatting | bytes 1048576
